TPU v7x, 256 devices: a whole 4x4x8 slice. The times are simulated.
256 devices in a mesh: ctx: 32 (over z, x_hi, core), tp: 8 (over x_lo, y).
Axes of the slice: x: 4 (x_hi: 2, x_lo: 2; x = x_hi * 2 + x_lo), y: 4, z: 8, core: 2. Of those that a mesh axis runs over, the one named last changes fastest.
Arguments:
- queries: bfloat16 [1, 8192, 8192], P(None, 'ctx', 'tp'), may hold values from -8 to 8
- keys: bfloat16 [1, 8192, 1024], P(None, 'ctx', 'tp'), may hold values from -5 to 5
- values: bfloat16 [1, 8192, 1024], P(None, 'ctx', 'tp'), may hold values from -6 to 6
Outputs:
- attended: bfloat16 [1, 8192, 8192], P(None, ('ctx', 'tp'))
All inputs are finite; a program needn't handle non-finite values.
Results may differ from a plain program's by a relative error of at most 0.0075.
Values may be sent and summed in bfloat16 or wider, within the bound.
A program may use at most 64 MiB of HBM per device.

v0:
```python
import math

import jax
import jax.numpy as jnp
from jax import lax
from jax.experimental import pallas as pl
from jax.experimental.pallas import tpu as pltpu
from jax.sharding import PartitionSpec as P

HD = 128
BLOCK = 1024
UNROLL = 4
SCALE = math.log2(math.e) / math.sqrt(HD)


def flash(q_ref, k_ref, v_ref, out_ref, best_ref, acc_ref):
    rows, width = q_ref.shape
    heads = width // HD
    row_start = lax.axis_index("ctx") * rows
    best_ref[...] = jnp.full_like(best_ref, -1e30)
    acc_ref[...] = jnp.zeros_like(acc_ref)

    def block(index, masked):
        start = pl.multiple_of(index * BLOCK, BLOCK)
        key = k_ref[pl.ds(start, BLOCK), :]
        value = jnp.concatenate(
            [v_ref[pl.ds(start, BLOCK), :], jnp.ones((BLOCK, HD), jnp.bfloat16)], axis=1
        )

        def head_group(group, carry):
            for u in range(UNROLL):
                head = group * UNROLL + u
                q = q_ref[:, pl.ds(pl.multiple_of(head * HD, HD), HD)]
                s = lax.dot_general(
                    q, key, (((1,), (1,)), ((), ())), preferred_element_type=jnp.float32
                )
                if masked:
                    row = row_start - start + lax.broadcasted_iota(jnp.int32, s.shape, 0)
                    col = lax.broadcasted_iota(jnp.int32, s.shape, 1)
                    s = jnp.where(col <= row, s, -1e30)
                old = best_ref[head]
                new = jnp.maximum(old, jnp.max(s, axis=1, keepdims=True))
                fade = jnp.exp2((old - new) * SCALE)
                p = jnp.exp2((s - new[:, :1]) * SCALE).astype(jnp.bfloat16)
                pv = jnp.dot(p, value, preferred_element_type=jnp.float32)
                acc_ref[head] = acc_ref[head] * jnp.concatenate([fade, fade], axis=1) + pv
                best_ref[head] = new
            return carry

        lax.fori_loop(0, heads // UNROLL, head_group, 0)

    last = row_start // BLOCK
    block(last, True)

    def full(index, carry):
        block(index, False)
        return carry

    lax.fori_loop(0, last, full, 0)
    for head in range(heads):
        acc = acc_ref[head]
        out_ref[:, head * HD : (head + 1) * HD] = (acc[:, :HD] / acc[:, HD:]).astype(jnp.bfloat16)


def local(queries, keys, values):
    _, rows, width = queries.shape
    heads = width // HD
    key_all = lax.all_gather(keys[0], "ctx", axis=0, tiled=True)
    value_all = lax.all_gather(values[0], "ctx", axis=0, tiled=True)
    attended = pl.pallas_call(
        flash,
        out_shape=jax.ShapeDtypeStruct((rows, width), jnp.bfloat16),
        in_specs=[pl.BlockSpec(memory_space=pltpu.VMEM)] * 3,
        out_specs=pl.BlockSpec(memory_space=pltpu.VMEM),
        scratch_shapes=[
            pltpu.VMEM((heads, rows, HD), jnp.float32),
            pltpu.VMEM((heads, rows, 2 * HD), jnp.float32),
        ],
        compiler_params=pltpu.CompilerParams(vmem_limit_bytes=48 * 2**20),
        name="flash",
    )(queries[0], key_all, value_all)
    return lax.all_to_all(attended[None], "tp", split_axis=1, concat_axis=2, tiled=True)


def solution(mesh):
    in_specs = (P(None, "ctx", "tp"), P(None, "ctx", "tp"), P(None, "ctx", "tp"))
    out_specs = P(None, ("ctx", "tp"), None)
    return jax.shard_map(local, mesh=mesh, in_specs=in_specs, out_specs=out_specs, check_vma=False)
```

profile of v0, /device:TPU:224, one launch (start us, length us, event | category | flops | bytes accessed | tf_op | source)
XLA Modules:
  0.0 232.5 jit_solution(3076386426894804016)
XLA Ops:
  6.5 0.0 all-gather.5.cloned.1.call-start
  6.5 0.7 all-gather.5.cloned.1.call-update
  7.3 0.0 all-gather.7.cloned.1.call-start
  7.3 0.7 all-gather.7.cloned.1.call-update
  8.0 80.9 %all-gather.5.cloned.1.call-done = bf16[1,8192,128]{2,1,0:T(8,128)(2,1)} async-done(((bf16[1,256,128]{2,1,0:T(8,128)(2,1)}), bf16[1,8192,128]{2,1,0:T(8,128)(2,1)}) %all-gather.5.cloned.1.call-update) | async-done | bytes 2097168 | tf_op jit(solution)/shard_map/all_gather | solution.py:68
  88.9 79.2 %all-gather.7.cloned.1.call-done = bf16[1,8192,128]{2,1,0:T(8,128)(2,1)} async-done(((bf16[1,256,128]{2,1,0:T(8,128)(2,1)}), bf16[1,8192,128]{2,1,0:T(8,128)(2,1)}) %all-gather.7.cloned.1.call-update) | async-done | bytes 2097168 | tf_op jit(solution)/shard_map/all_gather | solution.py:69
  168.1 0.0 copy-start
  168.1 1.6 copy-done
  169.7 0.0 copy-start.1
  169.7 1.6 copy-done.1
  171.3 0.0 copy-start.2
  171.3 1.0 copy-done.2
  172.3 31.8 %flash.1 = bf16[256,1024]{1,0:T(8,128)(2,1)S(1)} custom-call(bf16[256,1024]{1,0:T(8,128)(2,1)S(1)} %bitcast.16, bf16[8192,128]{1,0:T(8,128)(2,1)S(1)} %bitcast.14, bf16[8192,128]{1,0:T(8,128)(2,1)S(1)} %bitcast.15), custom_call_target="tpu_custom_call" | custom-call | tf_op jit(solution)/shard_map/flash/pallas_call | solution.py:70
  204.2 0.8 copy.13
  205.0 0.5 broadcast
  205.5 3.7 %reduce = bf16[256,1024]{1,0:T(8,128)(2,1)S(1)} reduce(bf16[256,1,1024]{2,1,0:T(2,128)(2,1)S(1)} %bitcast.18, bf16[]{:T(256)} %broadcast), dimensions={1}, to_apply=%bitcast.12.reduce_sub_computation | reduce | bytes 1048578
  209.2 0.4 reshape.2
  209.6 14.5 %all_to_all.18 = bf16[8,2,16384]{2,1,0:T(2,128)(2,1)S(1)} all-to-all(bf16[8,2,16384]{2,1,0:T(2,128)(2,1)S(1)} %reshape.2), channel_id=1, replica_groups=mesh['ctx'=32,'tp'=8] {'tp'}, dimensions={0} | all-to-all | bytes 1048576 | tf_op jit(solution)/shard_map/all_to_all | solution.py:82
  224.1 0.5 reshape.3
  224.6 0.2 copy.10
  224.8 0.8 copy.11
Async XLA Ops:
  6.5 82.4 %all-gather.5.cloned.1.call-start = ((), (), s32[]{:S(2)}) async-start(), calls=%async_computation.1 | async-start | bytes 2162688 | tf_op jit(solution)/shard_map/all_gather | solution.py:68
  7.3 160.8 %all-gather.7.cloned.1.call-start = ((), (), s32[]{:S(2)}) async-start(), calls=%async_computation.2 | async-start | bytes 2162688 | tf_op jit(solution)/shard_map/all_gather | solution.py:69
  168.1 1.6 copy-start
  169.7 1.6 copy-start.1
  171.3 1.0 copy-start.2
Sparse Core Ops, SparseCore 0:
  10.1 78.7 all-gather.4
  91.7 76.3 all-gather.6
where the time goes:
time: 233 us; the launch traced here: 232 us
  waiting for transfers between devices  161 us (69%)
  Pallas kernels  31.8 us (14%)
  blocking collectives  14.5 us (6%)
  between operations  13.4 us (6%)
  local copies, waits for them, and re-layouts  7.45 us (3%)
  other arithmetic  3.69 us (2%)
    all_gather x1, waiting for transfers between devices, local(): key_all = lax.all_gather(keys[0], 'ctx', axis=0, tiled=True)  80.9 us
    all_gather x1, waiting for transfers between devices, local(): value_all = lax.all_gather(values[0], 'ctx', axis=0, tiled=True)  79.2 us
    pallas_call x1, Pallas kernels, local(): pl.pallas_call(flash, out_shape=jax.ShapeDtypeStruct((rows, width), jnp.b...  31.8 us
    all_to_all x1, blocking collectives, local(): lax.all_to_all(attended[None], 'tp', split_axis=1, concat_axis=2, tiled=T...  14.5 us
    unnamed x10, local copies, waits for them, and re-layouts  5.8 us
  transfers between devices with their start and end apart: 2, of which 2 were waited for; matrix products, arithmetic and copies ran while one was open for 0% of the time, Pallas kernels for 0%

commit v1 on v0

v1 whole, which is shorter than its diff:
```python
import functools
import math

import jax
import jax.numpy as jnp
from jax import lax
from jax.experimental import pallas as pl
from jax.experimental.pallas import tpu as pltpu
from jax.sharding import PartitionSpec as P

HD = 128
UNROLL = 4
SCALE = math.log2(math.e) / math.sqrt(HD)
MESH = pl.DeviceIdType.MESH

PLANE = 4
UP, DOWN = 0, 1
NEAR, FAR = 0, 1


def kernel(
    planes,
    peers,
    q_hbm,
    k_hbm,
    v_hbm,
    out_ref,
    q_ref,
    kv_ref,
    best_ref,
    acc_ref,
    stage_ref,
    load_sem,
    x_sem,
    ring_send,
    ring_recv,
    core_send,
    core_recv,
    out_send,
    out_recv,
    own_sem,
):
    rows, width = q_ref.shape
    block_rows = PLANE * rows
    heads = width // HD
    groups = heads // UNROLL
    part = rows // peers
    reach = planes // 2
    me = lax.axis_index("ctx")
    tp = lax.axis_index("tp")
    z, x, core = me // PLANE, (me // 2) % 2, me % 2

    def slot(plane, col, c):
        return plane * PLANE + (x if col == NEAR else 1 - x) * 2 + c

    def beside(d, step):
        return lax.rem(z + planes - step if d == UP else z + step, planes)

    neighbour = (
        lax.rem(z + 1, planes) * PLANE + x * 2 + core,
        lax.rem(z + planes - 1, planes) * PLANE + x * 2 + core,
    )
    x_partner = z * PLANE + (1 - x) * 2 + core
    core_partner = z * PLANE + x * 2 + 1 - core

    def last(d, col):
        return reach if (d == UP) == (col == NEAR) else reach - 1

    def remote(index, send, recv, target):
        return pltpu.make_async_remote_copy(
            src_ref=kv_ref.at[index],
            dst_ref=kv_ref.at[index],
            send_sem=send,
            recv_sem=recv,
            device_id={"ctx": target},
            device_id_type=MESH,
        )

    def hop(d, col, step):
        return remote(
            slot(beside(d, step), col, core),
            ring_send.at[d, col, step],
            ring_recv.at[d, col, step + 1],
            neighbour[d],
        )

    def across(d, col, step, c):
        return remote(
            slot(beside(d, step), col, c),
            core_send.at[d, col, step],
            core_recv.at[d, col, step],
            core_partner,
        )

    def arrive(d, col, step):
        remote(
            slot(beside(d, step), col, core),
            ring_send.at[d, col, step],
            ring_recv.at[d, col, step],
            neighbour[d],
        ).wait_recv()

        @pl.when(step < last(d, col))
        def _():
            hop(d, col, step).start()

        across(d, col, step, core).start()

    def arrive_both(col, step):
        for d in (UP, DOWN):

            @pl.when(step <= last(d, col))
            def _():
                arrive(d, col, step)

    loads = [
        pltpu.make_async_copy(k_hbm, kv_ref.at[me, 0], load_sem.at[0]),
        pltpu.make_async_copy(v_hbm, kv_ref.at[me, 1], load_sem.at[1]),
        pltpu.make_async_copy(q_hbm, q_ref, load_sem.at[2]),
    ]
    for load in loads:
        load.start()
    barrier = pltpu.get_barrier_semaphore()
    for target in (*neighbour, x_partner, core_partner):
        pl.semaphore_signal(barrier, inc=1, device_id={"ctx": target}, device_id_type=MESH)
    for j in range(1, peers):
        pl.semaphore_signal(
            barrier, inc=1, device_id={"tp": lax.rem(tp + j, peers)}, device_id_type=MESH
        )
    loads[0].wait()
    loads[1].wait()
    pl.semaphore_wait(barrier, 4 + peers - 1)

    x_copy = remote(me, x_sem.at[0], x_sem.at[1], x_partner)
    x_copy.start()
    for d in (UP, DOWN):
        hop(d, NEAR, 0).start()
    across(UP, NEAR, 0, core).start()
    best_ref[...] = jnp.full_like(best_ref, -1e30)
    acc_ref[...] = jnp.zeros_like(acc_ref)
    arrive_both(NEAR, 1)
    remote(x_partner, x_sem.at[0], x_sem.at[1], x_partner).wait_recv()
    for d in (UP, DOWN):
        hop(d, FAR, 0).start()
    across(UP, FAR, 0, core).start()
    across(UP, NEAR, 0, 1 - core).wait_recv()
    across(UP, FAR, 0, 1 - core).wait_recv()
    loads[2].wait()

    def attend(plane, group, masked):
        held = kv_ref.at[pl.ds(plane * PLANE, PLANE)]
        key = held[:, 0].reshape(block_rows, HD)
        value = jnp.concatenate(
            [held[:, 1].reshape(block_rows, HD), jnp.ones((block_rows, HD), jnp.bfloat16)], axis=1
        )
        for u in range(UNROLL):
            head = group * UNROLL + u
            q = q_ref[:, pl.ds(pl.multiple_of(head * HD, HD), HD)]
            s = lax.dot_general(q, key, (((1,), (1,)), ((), ())), preferred_element_type=jnp.float32)
            if masked:
                row = (me - plane * PLANE) * rows + lax.broadcasted_iota(jnp.int32, s.shape, 0)
                col = lax.broadcasted_iota(jnp.int32, s.shape, 1)
                s = jnp.where(col <= row, s, -1e30)
            old = best_ref[head]
            new = jnp.maximum(old, jnp.max(s, axis=1, keepdims=True))
            fade = jnp.exp2((old - new) * SCALE)
            p = jnp.exp2((s - new[:, :1]) * SCALE).astype(jnp.bfloat16)
            pv = jnp.dot(p, value, preferred_element_type=jnp.float32)
            acc_ref[head] = acc_ref[head] * jnp.concatenate([fade, fade], axis=1) + pv
            best_ref[head] = new

    def own(group, carry):
        @pl.when(group == 0)
        def _():
            arrive_both(NEAR, 2)

        @pl.when(group == groups - 1)
        def _():
            arrive_both(FAR, 1)

        attend(z, group, True)
        return carry

    lax.fori_loop(0, groups, own, 0)

    def attend_step(step, carry):
        def attend_side(d, carry):
            @pl.when(d == 0)
            def _():
                arrive_both(NEAR, step + 2)
                for col in (NEAR, FAR):
                    across(UP, col, step, 1 - core).wait_recv()

            @pl.when(d == 1)
            def _():
                arrive_both(FAR, step + 1)
                for col in (NEAR, FAR):
                    across(DOWN, col, step, 1 - core).wait_recv()

            plane = lax.rem(z + planes + (2 * d - 1) * step, planes)

            @pl.when(plane < z)
            def _():
                def each(group, carry):
                    attend(plane, group, False)
                    return carry

                lax.fori_loop(0, groups, each, 0)

            return carry

        return lax.fori_loop(0, 2, attend_side, carry)

    lax.fori_loop(1, reach, attend_step, 0)
    across(UP, NEAR, reach, 1 - core).wait_recv()
    across(DOWN, FAR, reach, 1 - core).wait_recv()

    cut = UNROLL * HD

    def give(group, j, to, column):
        return pltpu.make_async_remote_copy(
            src_ref=stage_ref.at[
                pl.ds(pl.multiple_of(to * part, part), part),
                pl.ds(pl.multiple_of(group * cut, cut), cut),
            ],
            dst_ref=out_ref.at[:, pl.ds(pl.multiple_of(column * width + group * cut, cut), cut)],
            send_sem=out_send.at[group, j],
            recv_sem=out_recv.at[group, j],
            device_id={"tp": to},
            device_id_type=MESH,
        )

    def keep(group):
        return pltpu.make_async_copy(
            stage_ref.at[
                pl.ds(pl.multiple_of(tp * part, part), part),
                pl.ds(pl.multiple_of(group * cut, cut), cut),
            ],
            out_ref.at[:, pl.ds(pl.multiple_of(tp * width + group * cut, cut), cut)],
            own_sem.at[group],
        )

    def finish(group, carry):
        @pl.when(z >= reach)
        def _():
            attend(z - reach, group, False)

        for u in range(UNROLL):
            head = group * UNROLL + u
            acc = acc_ref[head]
            stage_ref[:, pl.ds(pl.multiple_of(head * HD, HD), HD)] = (
                acc[:, :HD] / acc[:, HD:]
            ).astype(jnp.bfloat16)
        for j in range(1, peers):
            give(group, j, lax.rem(tp + j, peers), tp).start()
        keep(group).start()
        return carry

    lax.fori_loop(0, groups, finish, 0)

    x_copy.wait_send()
    for d in (UP, DOWN):
        for col in (NEAR, FAR):
            for step in range(last(d, col) + 1):
                if step < last(d, col):
                    hop(d, col, step).wait_send()
                if step > 0 or d == UP:
                    across(d, col, step, core).wait_send()
    for group in range(groups):
        for j in range(1, peers):
            copy = give(group, j, lax.rem(tp + j, peers), lax.rem(tp + peers - j, peers))
            copy.wait_send()
            copy.wait_recv()
        keep(group).wait()


def local(planes, peers, queries, keys, values):
    _, rows, width = queries.shape
    heads = width // HD
    groups = heads // UNROLL
    steps = planes // 2 + 1
    dma = pltpu.SemaphoreType.DMA
    out = pl.pallas_call(
        functools.partial(kernel, planes, peers),
        out_shape=jax.ShapeDtypeStruct((rows // peers, width * peers), jnp.bfloat16),
        in_specs=[pl.BlockSpec(memory_space=pl.ANY)] * 3,
        out_specs=pl.BlockSpec(memory_space=pltpu.VMEM),
        scratch_shapes=[
            pltpu.VMEM((rows, width), jnp.bfloat16),
            pltpu.VMEM((planes * PLANE, 2, rows, HD), jnp.bfloat16),
            pltpu.VMEM((heads, rows, HD), jnp.float32),
            pltpu.VMEM((heads, rows, 2 * HD), jnp.float32),
            pltpu.VMEM((rows, width), jnp.bfloat16),
            dma((3,)),
            dma((2,)),
            dma((2, 2, steps)),
            dma((2, 2, steps)),
            dma((2, 2, steps)),
            dma((2, 2, steps)),
            dma((groups, peers)),
            dma((groups, peers)),
            dma((groups,)),
        ],
        compiler_params=pltpu.CompilerParams(
            vmem_limit_bytes=48 * 2**20, collective_id=0, has_side_effects=True
        ),
        name="ring_attention",
    )(queries[0], keys[0], values[0])
    return out[None]


def solution(mesh):
    in_specs = (P(None, "ctx", "tp"), P(None, "ctx", "tp"), P(None, "ctx", "tp"))
    out_specs = P(None, ("ctx", "tp"), None)
    planes, peers = mesh.shape["ctx"] // PLANE, mesh.shape["tp"]
    return jax.shard_map(
        functools.partial(local, planes, peers),
        mesh=mesh,
        in_specs=in_specs,
        out_specs=out_specs,
        check_vma=False,
    )
```

time: 233 us -> 57.7 us (0.25)
  waiting for transfers between devices: 161 us -> 0 us
  Pallas kernels: 31.8 us -> 53.9 us
  blocking collectives: 14.5 us -> 0 us
  between operations: 13.4 us -> 0.01 us
  local copies, waits for them, and re-layouts: 7.45 us -> 3.51 us
  other arithmetic: 3.69 us -> 0 us
    all_gather x2 -> x0, waiting for transfers between devices: 160 us -> none  [the longest x1 80.9 us: local(): key_all = lax.all_gather(keys[0], 'ctx', axis=0, tiled=True)]
    pallas_call x1, Pallas kernels: 31.8 us -> 53.9 us  [local(): pl.pallas_call(functools.partial(kernel, planes, peers), out_shape=jax.Sh...]
    all_to_all x1 -> x0, blocking collectives: 14.5 us -> none  [local(): lax.all_to_all(attended[None], 'tp', split_axis=1, concat_axis=2, tiled=T...]
    unnamed x1 -> x0, other arithmetic: 3.69 us -> none
    unnamed x10 -> x7, local copies, waits for them, and re-layouts: 5.8 us -> 3.51 us
  transfers between devices with their start and end apart: 2 -> 0, of which waited for: 2 -> 0; matrix products, arithmetic and copies ran while one was open for 0% -> 0% of each run, Pallas kernels for 0% -> 0%
where the time goes in v1:
time: 57.7 us; the launch traced here: 57.4 us
  Pallas kernels  53.9 us (93%)
  local copies, waits for them, and re-layouts  3.51 us (6%)
    pallas_call x1, Pallas kernels, local(): pl.pallas_call(functools.partial(kernel, planes, peers), out_shape=jax.Sh...  53.9 us
    unnamed x7, local copies, waits for them, and re-layouts  3.51 us

profile of v1, /device:TPU:224, one launch (start us, length us, event | category | flops | bytes accessed | tf_op | source)
XLA Modules:
  0.0 57.4 jit_solution(15041465279928159274)
XLA Ops:
  0.0 0.0 copy-start
  0.0 1.0 %copy-done = bf16[1,256,1024]{2,1,0:T(8,128)(2,1)S(1)} copy-done((bf16[1,256,1024]{2,1,0:T(8,128)(2,1)S(1)}, bf16[1,256,1024]{2,1,0:T(8,128)(2,1)}, u32[]{:S(2)}) %copy-start) | copy-done | bytes 524312
  1.0 0.0 copy-start.1
  1.0 0.8 %copy-done.1 = bf16[1,256,128]{2,1,0:T(8,128)(2,1)S(1)} copy-done((bf16[1,256,128]{2,1,0:T(8,128)(2,1)S(1)}, bf16[1,256,128]{2,1,0:T(8,128)(2,1)}, u32[]{:S(2)}) %copy-start.1) | copy-done | bytes 65560
  1.9 0.0 copy-start.2
  1.9 0.8 %copy-done.2 = bf16[1,256,128]{2,1,0:T(8,128)(2,1)S(1)} copy-done((bf16[1,256,128]{2,1,0:T(8,128)(2,1)S(1)}, bf16[1,256,128]{2,1,0:T(8,128)(2,1)}, u32[]{:S(2)}) %copy-start.2) | copy-done | bytes 65560
  2.7 53.9 %ring_attention.1 = bf16[32,8192]{1,0:T(8,128)(2,1)S(1)} custom-call(bf16[256,1024]{1,0:T(8,128)(2,1)S(1)} %bitcast.5, bf16[256,128]{1,0:T(8,128)(2,1)S(1)} %bitcast.6, bf16[256,128]{1,0:T(8,128)(2,1)S(1)} %bitcast.7), custom_call_target="tpu_custom_call" | custom-call | tf_op jit(solution)/shard_map/ring_attention/pallas_call | solution.py:283
  56.6 0.8 %copy.5 = bf16[1,32,8192]{2,1,0:T(8,128)(2,1)} copy(bf16[1,32,8192]{2,1,0:T(8,128)(2,1)S(1)} %bitcast.4) | data formatting | bytes 1048576
Async XLA Ops:
  0.0 1.0 %copy-start = (bf16[1,256,1024]{2,1,0:T(8,128)(2,1)S(1)}, bf16[1,256,1024]{2,1,0:T(8,128)(2,1)}, u32[]{:S(2)}) copy-start(bf16[1,256,1024]{2,1,0:T(8,128)(2,1)} %param.3) | copy-start | bytes 1572868
  1.0 0.8 %copy-start.1 = (bf16[1,256,128]{2,1,0:T(8,128)(2,1)S(1)}, bf16[1,256,128]{2,1,0:T(8,128)(2,1)}, u32[]{:S(2)}) copy-start(bf16[1,256,128]{2,1,0:T(8,128)(2,1)} %param.4) | copy-start | bytes 196612
  1.9 0.8 %copy-start.2 = (bf16[1,256,128]{2,1,0:T(8,128)(2,1)S(1)}, bf16[1,256,128]{2,1,0:T(8,128)(2,1)}, u32[]{:S(2)}) copy-start(bf16[1,256,128]{2,1,0:T(8,128)(2,1)} %param.5) | copy-start | bytes 196612

commit v2 on v1

--- a/solution.py
+++ b/solution.py
@@ -41,7 +41,6 @@
     own_sem,
 ):
     rows, width = q_ref.shape
-    block_rows = PLANE * rows
     heads = width // HD
     groups = heads // UNROLL
     part = rows // peers
@@ -65,6 +64,18 @@
 
     def last(d, col):
         return reach if (d == UP) == (col == NEAR) else reach - 1
+
+    def needed(d, step, at):
+        return at >= step if d == UP else at + step >= planes
+
+    def carried(d, col, step, at):
+        if d == UP:
+            return needed(d, step, at)
+        return needed(d, step, at) | (at + step + 1 <= last(d, col))
+
+    def passes(d, col, step):
+        at = lax.rem(z + 1 if d == UP else z + planes - 1, planes)
+        return (step < last(d, col)) & carried(d, col, step + 1, at)
 
     def remote(index, send, recv, target):
         return pltpu.make_async_remote_copy(
@@ -100,18 +111,35 @@
             neighbour[d],
         ).wait_recv()
 
-        @pl.when(step < last(d, col))
+        @pl.when(passes(d, col, step))
         def _():
             hop(d, col, step).start()
 
-        across(d, col, step, core).start()
+        @pl.when(needed(d, step, z))
+        def _():
+            across(d, col, step, core).start()
 
     def arrive_both(col, step):
         for d in (UP, DOWN):
 
-            @pl.when(step <= last(d, col))
+            @pl.when((step <= last(d, col)) & carried(d, col, step, z))
             def _():
                 arrive(d, col, step)
+
+    def begin(col):
+        for d in (UP, DOWN):
+
+            @pl.when(passes(d, col, 0))
+            def _():
+                hop(d, col, 0).start()
+
+        across(UP, col, 0, core).start()
+
+    def whole(d, step):
+        @pl.when(needed(d, step, z))
+        def _():
+            for col in (NEAR, FAR):
+                across(d, col, step, 1 - core).wait_recv()
 
     loads = [
         pltpu.make_async_copy(k_hbm, kv_ref.at[me, 0], load_sem.at[0]),
@@ -133,22 +161,13 @@
 
     x_copy = remote(me, x_sem.at[0], x_sem.at[1], x_partner)
     x_copy.start()
-    for d in (UP, DOWN):
-        hop(d, NEAR, 0).start()
-    across(UP, NEAR, 0, core).start()
+    begin(NEAR)
     best_ref[...] = jnp.full_like(best_ref, -1e30)
     acc_ref[...] = jnp.zeros_like(acc_ref)
-    arrive_both(NEAR, 1)
-    remote(x_partner, x_sem.at[0], x_sem.at[1], x_partner).wait_recv()
-    for d in (UP, DOWN):
-        hop(d, FAR, 0).start()
-    across(UP, FAR, 0, core).start()
-    across(UP, NEAR, 0, 1 - core).wait_recv()
-    across(UP, FAR, 0, 1 - core).wait_recv()
-    loads[2].wait()
-
-    def attend(plane, group, masked):
-        held = kv_ref.at[pl.ds(plane * PLANE, PLANE)]
+
+    def attend(first, count, group, masked):
+        held = kv_ref.at[pl.ds(first, count)]
+        block_rows = count * rows
         key = held[:, 0].reshape(block_rows, HD)
         value = jnp.concatenate(
             [held[:, 1].reshape(block_rows, HD), jnp.ones((block_rows, HD), jnp.bfloat16)], axis=1
@@ -158,7 +177,7 @@
             q = q_ref[:, pl.ds(pl.multiple_of(head * HD, HD), HD)]
             s = lax.dot_general(q, key, (((1,), (1,)), ((), ())), preferred_element_type=jnp.float32)
             if masked:
-                row = (me - plane * PLANE) * rows + lax.broadcasted_iota(jnp.int32, s.shape, 0)
+                row = (me - first) * rows + lax.broadcasted_iota(jnp.int32, s.shape, 0)
                 col = lax.broadcasted_iota(jnp.int32, s.shape, 1)
                 s = jnp.where(col <= row, s, -1e30)
             old = best_ref[head]
@@ -169,51 +188,68 @@
             acc_ref[head] = acc_ref[head] * jnp.concatenate([fade, fade], axis=1) + pv
             best_ref[head] = new
 
-    def own(group, carry):
-        @pl.when(group == 0)
-        def _():
-            arrive_both(NEAR, 2)
-
+    def near(group, carry):
         @pl.when(group == groups - 1)
         def _():
+            arrive_both(NEAR, 1)
+
+        attend(me - core, 2, group, True)
+        return carry
+
+    def far(group, carry):
+        @pl.when(group == groups - 1)
+        def _():
             arrive_both(FAR, 1)
 
-        attend(z, group, True)
+        @pl.when(x == 1)
+        def _():
+            attend(z * PLANE, 2, group, False)
+
         return carry
 
-    lax.fori_loop(0, groups, own, 0)
+    across(UP, NEAR, 0, 1 - core).wait_recv()
+    loads[2].wait()
+    lax.fori_loop(0, groups, near, 0)
+    remote(x_partner, x_sem.at[0], x_sem.at[1], x_partner).wait_recv()
+    begin(FAR)
+    arrive_both(NEAR, 2)
+    across(UP, FAR, 0, 1 - core).wait_recv()
+    lax.fori_loop(0, groups, far, 0)
 
     def attend_step(step, carry):
         def attend_side(d, carry):
             @pl.when(d == 0)
             def _():
                 arrive_both(NEAR, step + 2)
-                for col in (NEAR, FAR):
-                    across(UP, col, step, 1 - core).wait_recv()
+                whole(UP, step)
 
             @pl.when(d == 1)
             def _():
-                arrive_both(FAR, step + 1)
-                for col in (NEAR, FAR):
-                    across(DOWN, col, step, 1 - core).wait_recv()
+                whole(DOWN, step)
 
             plane = lax.rem(z + planes + (2 * d - 1) * step, planes)
 
-            @pl.when(plane < z)
-            def _():
-                def each(group, carry):
-                    attend(plane, group, False)
-                    return carry
-
-                lax.fori_loop(0, groups, each, 0)
-
-            return carry
+            def each(group, carry):
+                @pl.when((d == 0) & (group == groups - 1))
+                def _():
+                    arrive_both(FAR, step + 1)
+
+                @pl.when(plane < z)
+                def _():
+                    attend(plane * PLANE, PLANE, group, False)
+
+                return carry
+
+            return lax.fori_loop(0, groups, each, carry)
 
         return lax.fori_loop(0, 2, attend_side, carry)
 
     lax.fori_loop(1, reach, attend_step, 0)
-    across(UP, NEAR, reach, 1 - core).wait_recv()
-    across(DOWN, FAR, reach, 1 - core).wait_recv()
+
+    @pl.when(z >= reach)
+    def _():
+        across(UP, NEAR, reach, 1 - core).wait_recv()
+        across(DOWN, FAR, reach, 1 - core).wait_recv()
 
     cut = UNROLL * HD
 
@@ -243,7 +279,7 @@
     def finish(group, carry):
         @pl.when(z >= reach)
         def _():
-            attend(z - reach, group, False)
+            attend((z - reach) * PLANE, PLANE, group, False)
 
         for u in range(UNROLL):
             head = group * UNROLL + u
@@ -259,13 +295,20 @@
     lax.fori_loop(0, groups, finish, 0)
 
     x_copy.wait_send()
+    for col in (NEAR, FAR):
+        across(UP, col, 0, core).wait_send()
     for d in (UP, DOWN):
         for col in (NEAR, FAR):
             for step in range(last(d, col) + 1):
-                if step < last(d, col):
+                @pl.when(passes(d, col, step))
+                def _():
                     hop(d, col, step).wait_send()
-                if step > 0 or d == UP:
-                    across(d, col, step, core).wait_send()
+
+                if step > 0:
+
+                    @pl.when(needed(d, step, z))
+                    def _():
+                        across(d, col, step, core).wait_send()
     for group in range(groups):
         for j in range(1, peers):
             copy = give(group, j, lax.rem(tp + j, peers), lax.rem(tp + peers - j, peers))
@@ -283,8 +326,8 @@
     out = pl.pallas_call(
         functools.partial(kernel, planes, peers),
         out_shape=jax.ShapeDtypeStruct((rows // peers, width * peers), jnp.bfloat16),
-        in_specs=[pl.BlockSpec(memory_space=pl.ANY)] * 3,
-        out_specs=pl.BlockSpec(memory_space=pltpu.VMEM),
+        in_specs=[pl.BlockSpec(memory_space=pltpu.HBM)] * 3,
+        out_specs=pl.BlockSpec(memory_space=pltpu.HBM),
         scratch_shapes=[
             pltpu.VMEM((rows, width), jnp.bfloat16),
             pltpu.VMEM((planes * PLANE, 2, rows, HD), jnp.bfloat16),
@@ -302,7 +345,7 @@
             dma((groups,)),
         ],
         compiler_params=pltpu.CompilerParams(
-            vmem_limit_bytes=48 * 2**20, collective_id=0, has_side_effects=True
+            vmem_limit_bytes=67043328, collective_id=0, has_side_effects=True
         ),
         name="ring_attention",
     )(queries[0], keys[0], values[0])

time: 57.7 us -> 55.7 us (0.965)
  local copies, waits for them, and re-layouts: 3.51 us -> 1.87 us
    unnamed x7 -> x1, local copies, waits for them, and re-layouts: 3.51 us -> 1.87 us
where the time goes in v2:
time: 55.7 us; the launch traced here: 55.6 us
  Pallas kernels  53.7 us (96%)
  local copies, waits for them, and re-layouts  1.87 us (3%)
    pallas_call x1, Pallas kernels, local(): pl.pallas_call(functools.partial(kernel, planes, peers), out_shape=jax.Sh...  53.7 us
    unnamed x1, local copies, waits for them, and re-layouts  1.87 us

profile of v2, /device:TPU:224, one launch (start us, length us, event | category | flops | bytes accessed | tf_op | source)
XLA Modules:
  0.0 55.6 jit_solution(3747623937196441891)
XLA Ops:
  0.0 53.7 %ring_attention.1 = bf16[32,8192]{1,0:T(8,128)(2,1)} custom-call(bf16[256,1024]{1,0:T(8,128)(2,1)} %bitcast.5, bf16[256,128]{1,0:T(8,128)(2,1)} %bitcast.6, bf16[256,128]{1,0:T(8,128)(2,1)} %bitcast.7), custom_call_target="tpu_custom_call" | custom-call | tf_op jit(solution)/shard_map/ring_attention/pallas_call | solution.py:326
  53.7 1.9 %copy.5 = bf16[1,32,8192]{2,1,0:T(8,128)(2,1)} copy(bf16[1,32,8192]{2,1,0:T(8,128)(2,1)} %bitcast.4) | data formatting | bytes 1048576

commit v3 on v2

--- a/solution.py
+++ b/solution.py
@@ -183,7 +183,7 @@
             old = best_ref[head]
             new = jnp.maximum(old, jnp.max(s, axis=1, keepdims=True))
             fade = jnp.exp2((old - new) * SCALE)
-            p = jnp.exp2((s - new[:, :1]) * SCALE).astype(jnp.bfloat16)
+            p = jnp.exp2(s * SCALE - (new * SCALE)[:, :1]).astype(jnp.bfloat16)
             pv = jnp.dot(p, value, preferred_element_type=jnp.float32)
             acc_ref[head] = acc_ref[head] * jnp.concatenate([fade, fade], axis=1) + pv
             best_ref[head] = new

time: 55.7 us -> 56 us (level)
  no operation moved by 1% of the time
where the time goes in v3:
time: 56 us; the launch traced here: 55.9 us
  Pallas kernels  54 us (96%)
  local copies, waits for them, and re-layouts  1.87 us (3%)
    pallas_call x1, Pallas kernels, local(): pl.pallas_call(functools.partial(kernel, planes, peers), out_shape=jax.Sh...  54 us
    unnamed x1, local copies, waits for them, and re-layouts  1.87 us

profile of v3, /device:TPU:224, one launch (start us, length us, event | category | flops | bytes accessed | tf_op | source)
XLA Modules:
  0.0 55.9 jit_solution(4996040864459247621)
XLA Ops:
  0.0 54.0 %ring_attention.1 = bf16[32,8192]{1,0:T(8,128)(2,1)} custom-call(bf16[256,1024]{1,0:T(8,128)(2,1)} %bitcast.5, bf16[256,128]{1,0:T(8,128)(2,1)} %bitcast.6, bf16[256,128]{1,0:T(8,128)(2,1)} %bitcast.7), custom_call_target="tpu_custom_call" | custom-call | tf_op jit(solution)/shard_map/ring_attention/pallas_call | solution.py:326
  54.0 1.9 %copy.5 = bf16[1,32,8192]{2,1,0:T(8,128)(2,1)} copy(bf16[1,32,8192]{2,1,0:T(8,128)(2,1)} %bitcast.4) | data formatting | bytes 1048576
